TPU v7x, 32 devices: a whole 2x2x4 slice. The times are simulated.
32 devices in a mesh: groups: 2 (over y), space: 4 (over z), clus: 4 (over x, core).
Axes of the slice: x: 2, y: 2, z: 4, core: 2. Of those that a mesh axis runs over, the one named last changes fastest.
Arguments:
- snapshots: bfloat16 [256, 5, 49152], P('groups', None, ('space', 'clus')), parts along dimension 0
- labels: int32 [256], P('groups'), parts along dimension 0, may hold values from 0 to 3, as said below
- start: float32 [256, 16], P('groups'), parts along dimension 0, may hold values from -6 to 6
- successor: int32 [8], P('groups'), parts along dimension 0, may hold values from 0 to 3, as said below
Outputs:
- modes: bfloat16 [8, 16, 5, 49152], P(('groups', 'clus'), None, None, 'space'), parts along dimension 0
- coefficients: float32 [256, 16], P(('groups', 'clus')), parts along dimension 0
- correlations: float32 [8, 16, 16], P(('groups', 'clus')), parts along dimension 0
There are 2 independent parts, one for each index of `groups`. A program takes and returns all parts, laid end to end along the dimension named above; each array names one. Nothing has to cross between parts.
Inputs may be any that keep to these rules, and one draw needn't show every extreme that they name: `labels`: of the 32 snapshots of each aligned block (those of one index of clus), every cluster holds at least 6 and at most 8; in every block some cluster holds exactly 8. Following successor from any cluster visits all 4 clusters once before returning.
All inputs are finite; a program needn't handle non-finite values.
Results may differ from a plain program's by a relative error of at most 0.0045.
Values may be sent and summed in bfloat16 or wider, within the bound.
No kernel may reach another device: no remote copies, remote signals or barrier semaphores. Data moves between devices by JAX's collectives and lax.ppermute only.
A program may use at most 64 MiB of HBM per device.

v0:
```python
import jax
import jax.numpy as jnp
from jax import lax
from jax.sharding import PartitionSpec as P

ITERS = 2


def subspace(gram, member, start):
    basis = member[:, :, None] * start[None, :, :]
    for step in range(ITERS):
        image = (
            member[:, :, None]
            * jnp.einsum("st,ktm->ksm", gram, basis, precision=lax.Precision.HIGHEST)
            + basis
        )
        inner = jnp.einsum("ksm,ksn->kmn", image, image, precision=lax.Precision.HIGHEST)
        lower = jnp.linalg.cholesky(inner)
        basis = lax.linalg.triangular_solve(
            lower, image, left_side=False, lower=True, transpose_a=True
        )
    return basis


def local(snapshots, labels, start, successor):
    count, variables, cells = snapshots.shape
    clusters = lax.axis_size("clus")
    owner = lax.axis_index("clus")
    total_rows = variables * cells * lax.axis_size("space") * clusters
    flat = snapshots.reshape(count, variables * cells)
    partial_value = lax.dot_general(
        flat, flat, (((1,), (1,)), ((), ())), preferred_element_type=jnp.float32
    )
    gram = lax.psum(partial_value, ("space", "clus")) / total_rows
    cluster_ids = jnp.arange(clusters, dtype=jnp.int32)
    member = (labels[None, :] == cluster_ids[:, None]).astype(jnp.float32)
    basis = subspace(gram, member, start)
    picked = jnp.einsum("ks,ksm->sm", member, basis, precision=lax.Precision.HIGHEST)
    snap_dev = count // clusters
    coefficients = lax.dynamic_slice_in_dim(picked, owner * snap_dev, snap_dev, 0)
    rounded = basis.astype(jnp.bfloat16)
    mode_count = rounded.shape[2]
    modes_full = None
    left = jnp.transpose(rounded, (0, 2, 1)).reshape(clusters * mode_count, count)
    modes_full = jnp.dot(left, flat, preferred_element_type=jnp.float32)
    packed = modes_full.astype(jnp.bfloat16).reshape(clusters, mode_count, variables, cells)
    modes_out = lax.all_to_all(packed, "clus", split_axis=0, concat_axis=3, tiled=True)
    select = (successor[:, None] == cluster_ids[None, :]).astype(jnp.float32)
    wide = rounded.astype(jnp.float32)
    partner = jnp.einsum("ab,bsn->asn", select, wide, precision=lax.Precision.HIGHEST)
    image = jnp.einsum("st,atn->asn", gram, partner, precision=lax.Precision.HIGHEST)
    correlations = jnp.einsum("asm,asn->amn", wide, image, precision=lax.Precision.HIGHEST)
    own_correlation = lax.dynamic_slice_in_dim(correlations, owner, 1, 0)
    return (modes_out, coefficients, own_correlation)


def solution(mesh):
    in_specs = (P("groups", None, ("space", "clus")), P("groups"), P("groups", None), P("groups"))
    out_specs = (
        P(("groups", "clus"), None, None, "space"),
        P(("groups", "clus"), None),
        P(("groups", "clus"), None, None),
    )
    return jax.shard_map(local, mesh=mesh, in_specs=in_specs, out_specs=out_specs, check_vma=False)
```

profile of v0, /device:TPU:8, one launch (start us, length us, event | category | flops | bytes accessed | tf_op | source)
XLA Modules:
  0.0 174.2 jit_solution(173776694287602055)
XLA Ops:
  7.2 5.1 %convolution_bitcast_fusion = f32[128,128]{1,0:T(8,128)} fusion(bf16[128,5,3072]{2,0,1:T(8,128)(2,1)} %param.7), kind=kOutput, calls=%fused_computation.1 | convolution fusion | flops 503316480 | bytes 3997696 | tf_op jit(solution)/shard_map/dot_general | solution.py:31
  12.4 6.3 %copy.38 = bf16[128,5,3072]{0,2,1:T(8,128)(2,1)} copy(bf16[128,5,3072]{2,0,1:T(8,128)(2,1)} %param.7) | data formatting | bytes 7864320 | tf_op args[0]
  18.7 82.0 %all-reduce.2.cloned.1.call-done = f32[128,128]{1,0:T(8,128)} async-done(((f32[128,128]{1,0:T(8,128)}), f32[128,128]{1,0:T(8,128)}) %all-reduce.2.cloned.1.call-update) | async-done | bytes 65552 | tf_op jit(solution)/shard_map/psum | solution.py:34
  100.7 1.1 fusion.3
  101.8 0.2 fusion.35
  102.1 5.9 %custom-call.8 = f32[4,16,16]{2,1,0:T(8,128)S(1)} custom-call(f32[4,16,16]{2,1,0:T(8,128)S(1)} %fusion.16), custom_call_target="Cholesky" | custom-call | tf_op jit(solution)/shard_map/jit(cholesky)/cholesky | solution.py:18
  108.2 4.9 %custom-call.9 = f32[4,1,16,16]{2,3,1,0:T(8,128)S(1)} custom-call(f32[4,1,16,16]{3,2,1,0:T(8,128)S(1)} %select_bitcast_fusion.1), custom_call_target="InvertDiagBlocksLowerTriangular" | custom-call | tf_op jit(solution)/shard_map/triangular_solve/custom-call.0 | solution.py:19
  113.1 0.3 convolution_bitcast_fusion.1
  113.4 1.1 fusion.1
  114.5 0.2 fusion.36
  114.7 5.9 %custom-call.10 = f32[4,16,16]{2,1,0:T(8,128)S(1)} custom-call(f32[4,16,16]{2,1,0:T(8,128)S(1)} %fusion.14), custom_call_target="Cholesky" | custom-call | tf_op jit(solution)/shard_map/jit(cholesky)/cholesky | solution.py:18
  120.8 4.9 %custom-call.11 = f32[4,1,16,16]{2,3,1,0:T(8,128)S(1)} custom-call(f32[4,1,16,16]{3,2,1,0:T(8,128)S(1)} %select_bitcast_fusion), custom_call_target="InvertDiagBlocksLowerTriangular" | custom-call | tf_op jit(solution)/shard_map/triangular_solve/custom-call.0 | solution.py:19
  125.7 0.3 bitcast_convert_fusion
  126.0 4.9 %convolution_convert_fusion = bf16[64,15360]{1,0:T(8,128)(2,1)} fusion(bf16[64,128]{1,0:T(8,128)(2,1)S(1)} %bitcast.78, bf16[128,15360]{0,1:T(8,128)(2,1)} %bitcast.75), kind=kOutput, calls=%fused_computation | convolution fusion | flops 252641280 | bytes 5914624 | tf_op jit(solution)/shard_map/dot_general | solution.py:45
  130.9 4.6 %reshape.50 = bf16[4,16,5,3072]{3,2,1,0:T(8,128)(2,1)S(1)} reshape(bf16[64,15360]{1,0:T(8,128)(2,1)} %convolution_convert_fusion) | data formatting | bytes 3932160 | tf_op jit(solution)/shard_map/reshape | solution.py:46
  135.5 2.6 %copy.39 = bf16[4,16,5,3072]{3,1,2,0:T(8,128)(2,1)} copy(bf16[4,16,5,3072]{3,2,1,0:T(8,128)(2,1)S(1)} %reshape.50) | data formatting | bytes 3932160 | tf_op jit(solution)/shard_map/reshape | solution.py:46
  138.1 3.6 %all-to-all-start = ((bf16[4,16,5,3072]{3,1,2,0:T(8,128)(2,1)}), bf16[4,16,5,3072]{3,1,2,0:T(8,128)(2,1)S(1)}, u32[]{:S(2)}, u32[]{:S(2)}) async-start(bf16[4,16,5,3072]{3,1,2,0:T(8,128)(2,1)} %copy.39), calls=%async_computation | async-start | bytes 3932160 | tf_op jit(solution)/shard_map/all_to_all | solution.py:47
  141.7 0.7 constant_dynamic-slice_fusion.1
  142.4 0.2 fusion.22
  142.6 0.2 fusion.4
  142.8 0.1 fusion.37
  143.0 0.6 constant_dynamic-slice_fusion
  143.6 22.4 %all-to-all-done = bf16[4,16,5,3072]{3,1,2,0:T(8,128)(2,1)S(1)} async-done(((bf16[4,16,5,3072]{3,1,2,0:T(8,128)(2,1)}), bf16[4,16,5,3072]{3,1,2,0:T(8,128)(2,1)S(1)}, u32[]{:S(2)}, u32[]{:S(2)}) %all-to-all-start) | async-done | bytes 1966112 | tf_op jit(solution)/shard_map/all_to_all | solution.py:47
  165.9 1.4 copy.52
  (24 shorter events, 0.7 us)
Async XLA Ops:
  7.2 5.2 %copy-start.2 = (s32[128]{0:T(128)S(1)}, s32[128]{0:T(128)}, u32[]{:S(2)}) copy-start(s32[128]{0:T(128)} %param.8) | copy-start | bytes 1540
  7.2 93.5 %all-reduce.2.cloned.1.call-start = ((), (), s32[]{:S(2)}) async-start(), calls=%async_computation.1 | async-start | bytes 131072 | tf_op jit(solution)/shard_map/psum | solution.py:34
  12.4 88.3 %copy-start.1 = (f32[128,16]{0,1:T(8,128)S(1)}, f32[128,16]{0,1:T(8,128)}, u32[]{:S(2)}) copy-start(f32[128,16]{0,1:T(8,128)} %param.9) | copy-start | bytes 24580
  135.5 6.9 %copy-start.3 = (s32[4]{0:T(128)S(1)}, s32[4]{0:T(128)}, u32[]{:S(2)}) copy-start(s32[4]{0:T(128)} %param.10) | copy-start | bytes 52
  135.5 7.1 %copy-start = (f32[128,128]{1,0:T(8,128)S(1)}, f32[128,128]{1,0:T(8,128)}, u32[]{:S(2)}) copy-start(f32[128,128]{1,0:T(8,128)} %all-reduce.2.cloned.1.call-done) | copy-start | bytes 196612
  138.1 27.9 %all-to-all-start = ((bf16[4,16,5,3072]{3,1,2,0:T(8,128)(2,1)}), bf16[4,16,5,3072]{3,1,2,0:T(8,128)(2,1)S(1)}, u32[]{:S(2)}, u32[]{:S(2)}) async-start(bf16[4,16,5,3072]{3,1,2,0:T(8,128)(2,1)} %copy.39), calls=%async_computation | async-start | bytes 3932160 | tf_op jit(solution)/shard_map/all_to_all | solution.py:47
Sparse Core Ops, SparseCore 0:
  12.5 88.1 all-reduce.1
where the time goes:
time: 175 us; the launch traced here: 174 us
  waiting for transfers between devices  104 us (59%)
  other arithmetic  22.1 us (13%)
  local copies, waits for them, and re-layouts  16.3 us (9%)
  between operations  14.2 us (8%)
  matrix products  13.6 us (8%)
  starting transfers between devices  3.64 us (2%)
    psum x1, waiting for transfers between devices, local(): gram = lax.psum(partial_value, ('space', 'clus')) / total_rows  82 us
    all_to_all x1, waiting for transfers between devices, local(): lax.all_to_all(packed, 'clus', split_axis=0, concat_axis=3, tiled=True)  22.4 us
    another operation x7, other arithmetic, subspace(): lower = jnp.linalg.cholesky(inner)  12 us
    another operation x5, other arithmetic, subspace(): lax.linalg.triangular_solve(lower, image, left_side=False, lower=True, tr...  9.99 us
    reshape x2, local copies, waits for them, and re-layouts, local(): modes_full.astype(jnp.bfloat16)  7.12 us
    unnamed x9, local copies, waits for them, and re-layouts  6.29 us
    dot_general x1, matrix products, local(): lax.dot_general(flat, flat, (((1,), (1,)), ((), ())), preferred_element_t...  5.13 us
    dot_general x1, matrix products, local(): modes_full = jnp.dot(left, flat, preferred_element_type=jnp.float32)  4.86 us
  transfers between devices with their start and end apart: 2, of which 2 were waited for; matrix products, arithmetic and copies ran while one was open for 5% of the time, Pallas kernels for 0%

commit v1 on v0

--- a/solution.py
+++ b/solution.py
@@ -4,6 +4,11 @@
 from jax.sharding import PartitionSpec as P
 
 ITERS = 2
+
+
+def one_after_other(array, inner_axis, outer_axis):
+    partial = lax.psum(array, inner_axis)
+    return lax.psum(partial, outer_axis)
 
 
 def subspace(gram, member, start):
@@ -31,7 +36,7 @@
     partial_value = lax.dot_general(
         flat, flat, (((1,), (1,)), ((), ())), preferred_element_type=jnp.float32
     )
-    gram = lax.psum(partial_value, ("space", "clus")) / total_rows
+    gram = one_after_other(partial_value, "clus", "space") / total_rows
     cluster_ids = jnp.arange(clusters, dtype=jnp.int32)
     member = (labels[None, :] == cluster_ids[:, None]).astype(jnp.float32)
     basis = subspace(gram, member, start)

time: 175 us -> 157 us (0.90)
  waiting for transfers between devices: 104 us -> 84.7 us
    psum x1 -> x2, waiting for transfers between devices: 82 us -> 62.3 us  [the longest x1 36.3 us: one_after_other(): return lax.psum(partial, outer_axis)]
  transfers between devices with their start and end apart: 2 -> 3, of which waited for: 2 -> 3; matrix products, arithmetic and copies ran while one was open for 5% -> 5% of each run, Pallas kernels for 0% -> 0%
where the time goes in v1:
time: 157 us; the launch traced here: 155 us
  waiting for transfers between devices  84.7 us (54%)
  other arithmetic  22.1 us (14%)
  local copies, waits for them, and re-layouts  16.3 us (10%)
  between operations  14.2 us (9%)
  matrix products  13.7 us (9%)
  starting transfers between devices  3.68 us (2%)
    psum x1, waiting for transfers between devices, one_after_other(): return lax.psum(partial, outer_axis)  36.3 us
    psum x1, waiting for transfers between devices, one_after_other(): partial = lax.psum(array, inner_axis)  26 us
    all_to_all x1, waiting for transfers between devices, local(): lax.all_to_all(packed, 'clus', split_axis=0, concat_axis=3, tiled=True)  22.4 us
    another operation x7, other arithmetic, subspace(): lower = jnp.linalg.cholesky(inner)  12 us
    another operation x5, other arithmetic, subspace(): lax.linalg.triangular_solve(lower, image, left_side=False, lower=True, tr...  9.99 us
    reshape x2, local copies, waits for them, and re-layouts, local(): modes_full.astype(jnp.bfloat16)  7.12 us
    unnamed x9, local copies, waits for them, and re-layouts  6.29 us
    dot_general x1, matrix products, local(): lax.dot_general(flat, flat, (((1,), (1,)), ((), ())), preferred_element_t...  5.13 us
  transfers between devices with their start and end apart: 3, of which 3 were waited for; matrix products, arithmetic and copies ran while one was open for 5% of the time, Pallas kernels for 0%

profile of v1, /device:TPU:8, one launch (start us, length us, event | category | flops | bytes accessed | tf_op | source)
XLA Modules:
  0.0 154.6 jit_solution(17906495576228358992)
XLA Ops:
  7.2 5.1 %convolution_bitcast_fusion = f32[128,128]{1,0:T(8,128)} fusion(bf16[128,5,3072]{2,0,1:T(8,128)(2,1)} %param.7), kind=kOutput, calls=%fused_computation.1 | convolution fusion | flops 503316480 | bytes 3997696 | tf_op jit(solution)/shard_map/dot_general | solution.py:36
  12.5 6.3 %copy.38 = bf16[128,5,3072]{0,2,1:T(8,128)(2,1)} copy(bf16[128,5,3072]{2,0,1:T(8,128)(2,1)} %param.7) | data formatting | bytes 7864320 | tf_op args[0]
  18.7 26.0 %all-reduce.3.cloned.1.call-done = f32[128,128]{1,0:T(8,128)} async-done(((f32[128,128]{1,0:T(8,128)}), f32[128,128]{1,0:T(8,128)}) %all-reduce.3.cloned.1.call-update) | async-done | bytes 65552 | tf_op jit(solution)/shard_map/psum | solution.py:10
  44.8 36.3 %all-reduce.5.cloned.1.call-done = f32[128,128]{1,0:T(8,128)} async-done(((f32[128,128]{1,0:T(8,128)}), f32[128,128]{1,0:T(8,128)}) %all-reduce.5.cloned.1.call-update) | async-done | bytes 65552 | tf_op jit(solution)/shard_map/psum | solution.py:11
  81.1 1.1 fusion.3
  82.2 0.2 fusion.35
  82.5 5.9 %custom-call.8 = f32[4,16,16]{2,1,0:T(8,128)S(1)} custom-call(f32[4,16,16]{2,1,0:T(8,128)S(1)} %fusion.16), custom_call_target="Cholesky" | custom-call | tf_op jit(solution)/shard_map/jit(cholesky)/cholesky | solution.py:23
  88.5 4.9 %custom-call.9 = f32[4,1,16,16]{2,3,1,0:T(8,128)S(1)} custom-call(f32[4,1,16,16]{3,2,1,0:T(8,128)S(1)} %select_bitcast_fusion.1), custom_call_target="InvertDiagBlocksLowerTriangular" | custom-call | tf_op jit(solution)/shard_map/triangular_solve/custom-call.0 | solution.py:24
  93.5 0.3 convolution_bitcast_fusion.1
  93.8 1.1 fusion.1
  94.9 0.2 fusion.36
  95.1 5.9 %custom-call.10 = f32[4,16,16]{2,1,0:T(8,128)S(1)} custom-call(f32[4,16,16]{2,1,0:T(8,128)S(1)} %fusion.14), custom_call_target="Cholesky" | custom-call | tf_op jit(solution)/shard_map/jit(cholesky)/cholesky | solution.py:23
  101.2 4.9 %custom-call.11 = f32[4,1,16,16]{2,3,1,0:T(8,128)S(1)} custom-call(f32[4,1,16,16]{3,2,1,0:T(8,128)S(1)} %select_bitcast_fusion), custom_call_target="InvertDiagBlocksLowerTriangular" | custom-call | tf_op jit(solution)/shard_map/triangular_solve/custom-call.0 | solution.py:24
  106.1 0.3 bitcast_convert_fusion
  106.4 4.9 %convolution_convert_fusion = bf16[64,15360]{1,0:T(8,128)(2,1)} fusion(bf16[64,128]{1,0:T(8,128)(2,1)S(1)} %bitcast.78, bf16[128,15360]{0,1:T(8,128)(2,1)} %bitcast.75), kind=kOutput, calls=%fused_computation | convolution fusion | flops 252641280 | bytes 5914624 | tf_op jit(solution)/shard_map/dot_general | solution.py:50
  111.3 4.6 %reshape.50 = bf16[4,16,5,3072]{3,2,1,0:T(8,128)(2,1)S(1)} reshape(bf16[64,15360]{1,0:T(8,128)(2,1)} %convolution_convert_fusion) | data formatting | bytes 3932160 | tf_op jit(solution)/shard_map/reshape | solution.py:51
  115.9 2.6 %copy.39 = bf16[4,16,5,3072]{3,1,2,0:T(8,128)(2,1)} copy(bf16[4,16,5,3072]{3,2,1,0:T(8,128)(2,1)S(1)} %reshape.50) | data formatting | bytes 3932160 | tf_op jit(solution)/shard_map/reshape | solution.py:51
  118.5 3.6 %all-to-all-start = ((bf16[4,16,5,3072]{3,1,2,0:T(8,128)(2,1)}), bf16[4,16,5,3072]{3,1,2,0:T(8,128)(2,1)S(1)}, u32[]{:S(2)}, u32[]{:S(2)}) async-start(bf16[4,16,5,3072]{3,1,2,0:T(8,128)(2,1)} %copy.39), calls=%async_computation | async-start | bytes 3932160 | tf_op jit(solution)/shard_map/all_to_all | solution.py:52
  122.1 0.7 constant_dynamic-slice_fusion.1
  122.8 0.2 fusion.22
  123.0 0.2 fusion.4
  123.3 0.6 constant_dynamic-slice_fusion
  124.0 22.4 %all-to-all-done = bf16[4,16,5,3072]{3,1,2,0:T(8,128)(2,1)S(1)} async-done(((bf16[4,16,5,3072]{3,1,2,0:T(8,128)(2,1)}), bf16[4,16,5,3072]{3,1,2,0:T(8,128)(2,1)S(1)}, u32[]{:S(2)}, u32[]{:S(2)}) %all-to-all-start) | async-done | bytes 1966112 | tf_op jit(solution)/shard_map/all_to_all | solution.py:52
  146.3 1.4 copy.52
  (27 shorter events, 0.9 us)
Async XLA Ops:
  7.2 5.3 %copy-start.2 = (s32[128]{0:T(128)S(1)}, s32[128]{0:T(128)}, u32[]{:S(2)}) copy-start(s32[128]{0:T(128)} %param.8) | copy-start | bytes 1540
  7.2 37.5 %all-reduce.3.cloned.1.call-start = ((), (), s32[]{:S(2)}) async-start(), calls=%async_computation.1 | async-start | bytes 131072 | tf_op jit(solution)/shard_map/psum | solution.py:10
  12.4 68.7 %all-reduce.5.cloned.1.call-start = ((), (), s32[]{:S(2)}) async-start(), calls=%async_computation.2 | async-start | bytes 131072 | tf_op jit(solution)/shard_map/psum | solution.py:11
  12.5 68.6 %copy-start.1 = (f32[128,16]{0,1:T(8,128)S(1)}, f32[128,16]{0,1:T(8,128)}, u32[]{:S(2)}) copy-start(f32[128,16]{0,1:T(8,128)} %param.9) | copy-start | bytes 24580
  115.9 6.9 %copy-start.3 = (s32[4]{0:T(128)S(1)}, s32[4]{0:T(128)}, u32[]{:S(2)}) copy-start(s32[4]{0:T(128)} %param.10) | copy-start | bytes 52
  115.9 7.1 %copy-start = (f32[128,128]{1,0:T(8,128)S(1)}, f32[128,128]{1,0:T(8,128)}, u32[]{:S(2)}) copy-start(f32[128,128]{1,0:T(8,128)} %all-reduce.5.cloned.1.call-done) | copy-start | bytes 196612
  118.5 27.9 %all-to-all-start = ((bf16[4,16,5,3072]{3,1,2,0:T(8,128)(2,1)}), bf16[4,16,5,3072]{3,1,2,0:T(8,128)(2,1)S(1)}, u32[]{:S(2)}, u32[]{:S(2)}) async-start(bf16[4,16,5,3072]{3,1,2,0:T(8,128)(2,1)} %copy.39), calls=%async_computation | async-start | bytes 3932160 | tf_op jit(solution)/shard_map/all_to_all | solution.py:52
Sparse Core Ops, SparseCore 0:
  12.5 32.1 all-reduce.2
  47.1 33.9 all-reduce.4
